TPU v7x, 256 devices: a whole 4x4x8 slice. The times are simulated.
256 devices in a mesh: ctx: 64 (over y, z, core), head: 4 (over x).
Axes of the slice: x: 4, y: 4, z: 8, core: 2. Of those that a mesh axis runs over, the one named last changes fastest.
Arguments:
- query: bfloat16 [64, 2, 512, 4096], P('ctx', None, None, 'head'), may hold values from -48 to 48
- key: bfloat16 [64, 2, 512, 512], P('ctx', None, 'head'), may hold values from -18 to 18
- value: bfloat16 [64, 2, 512, 512], P('ctx', None, 'head'), may hold values from -6 to 6
- d_out: bfloat16 [64, 2, 512, 4096], P('ctx', None, None, 'head'), may hold values from -6 to 6
- doc_start: int32 [512], replicated, may hold values from 0 to 1, as said below
Outputs:
- d_query: bfloat16 [64, 2, 512, 4096], P('ctx', None, None, 'head')
- d_key: bfloat16 [64, 2, 512, 512], P('ctx', None, 'head')
- d_value: bfloat16 [64, 2, 512, 512], P('ctx', None, 'head')
Inputs may be any that keep to these rules, and one draw needn't show every extreme that they name: `doc_start`: 1 where a document begins at that block of 128 tokens (blocks in sequence order); block 0 begins one; from every beginning the next beginning, or the end of the sequence, is 1 to 3 blocks away; the first block of every span after the first lies inside a document of exactly 3 blocks that began in the span before.
All inputs are finite; a program needn't handle non-finite values.
Results may differ from a plain program's by a relative error of at most 0.039.
Values may be sent and summed in bfloat16 or wider, within the bound.
A program may use at most 64 MiB of HBM per device.

v0:
```python
import jax
import jax.numpy as jnp
from jax import lax
from jax.sharding import PartitionSpec as P

HD = 128
BLK = 128
GROUP = 8


def padded_2(cells, sides, width):
    for axis, dim in sides:
        count = lax.axis_size(axis)
        ends = count - 1
        head = lax.slice_in_dim(cells, 0, width, axis=dim)
        tail = lax.slice_in_dim(cells, cells.shape[dim] - width, cells.shape[dim], axis=dim)
        cells = jnp.concatenate(
            [
                lax.ppermute(tail, axis, [(i, (i + 1) % count) for i in range(ends)]),
                cells,
                lax.ppermute(head, axis, [((i + 1) % count, i) for i in range(ends)]),
            ],
            axis=dim,
        )
    return cells


def windowed(extended, reach_rows, blocks):
    pieces = []
    for offset in range(reach_rows // BLK + 1):
        sliced = lax.slice_in_dim(extended, offset * BLK, offset * BLK + blocks * BLK, axis=0)
        pieces.append(sliced.reshape((blocks, BLK) + extended.shape[1:]))
    return jnp.concatenate(pieces, axis=1)


def unwindowed(windows, reach_rows, blocks):
    summed = None
    for offset in range(reach_rows // BLK + 1):
        sliced = windows[:, offset * BLK : (offset + 1) * BLK].reshape(
            (blocks * BLK,) + windows.shape[2:]
        )
        padded = jnp.pad(
            sliced, ((offset * BLK, reach_rows - offset * BLK),) + ((0, 0),) * (windows.ndim - 2)
        )
        summed = padded if summed is None else summed + padded
    return summed


def span_grads(queries, grads_out, keys_ext, values_ext, doc_begins, span_start, reach_rows):
    blocks = queries.shape[0] // BLK
    kv_heads = keys_ext.shape[1] // HD
    score_scale = HD ** (-0.5)
    q_blocks = queries.reshape(blocks, BLK, kv_heads, GROUP, HD)
    do_blocks = grads_out.reshape(blocks, BLK, kv_heads, GROUP, HD)
    k_windows = windowed(keys_ext.reshape(-1, kv_heads, HD), reach_rows, blocks)
    v_windows = windowed(values_ext.reshape(-1, kv_heads, HD), reach_rows, blocks)
    row_pos = jnp.arange(BLK, dtype=jnp.int32)[None, :, None]
    col_pos = jnp.arange(reach_rows + BLK, dtype=jnp.int32)[None, None, :]
    key_pos = (
        span_start - reach_rows + jnp.arange(blocks, dtype=jnp.int32)[:, None, None] * BLK + col_pos
    )
    visible = (col_pos <= row_pos + reach_rows) & (key_pos >= doc_begins[:, None, None])
    visible = visible[:, None, None]
    scores = (
        jnp.einsum("btgjd,bkgd->bgjtk", q_blocks, k_windows, preferred_element_type=jnp.float32)
        * score_scale
    )
    peak = jnp.max(jnp.where(visible, scores, -1e30), axis=-1, keepdims=True)
    weights = jnp.exp(jnp.where(visible, scores - peak, -1e30))
    probs = weights / jnp.sum(weights, axis=-1, keepdims=True)
    probs_b = probs.astype(jnp.bfloat16)
    outputs = jnp.einsum(
        "bgjtk,bkgd->btgjd", probs_b, v_windows, preferred_element_type=jnp.float32
    ).astype(jnp.bfloat16)
    deltas = jnp.sum(do_blocks.astype(jnp.float32) * outputs.astype(jnp.float32), axis=-1)
    dprobs = jnp.einsum(
        "btgjd,bkgd->bgjtk", do_blocks, v_windows, preferred_element_type=jnp.float32
    )
    dscores = (
        probs * (dprobs - jnp.transpose(deltas, (0, 2, 3, 1))[..., None]) * score_scale
    ).astype(jnp.bfloat16)
    d_queries = jnp.einsum(
        "bgjtk,bkgd->btgjd", dscores, k_windows, preferred_element_type=jnp.float32
    ).astype(jnp.bfloat16)
    dk_windows = jnp.einsum(
        "bgjtk,btgjd->bkgd", dscores, q_blocks, preferred_element_type=jnp.float32
    )
    dv_windows = jnp.einsum(
        "bgjtk,btgjd->bkgd", probs_b, do_blocks, preferred_element_type=jnp.float32
    )
    return (
        d_queries.reshape(blocks * BLK, -1),
        unwindowed(dk_windows, reach_rows, blocks).reshape(-1, kv_heads * HD),
        unwindowed(dv_windows, reach_rows, blocks).reshape(-1, kv_heads * HD),
    )


def per_device(query, key, value, d_out, doc_start):
    kv_key, kv_value = (
        lax.all_to_all(key, "head", split_axis=3, concat_axis=2, tiled=True),
        lax.all_to_all(value, "head", split_axis=3, concat_axis=2, tiled=True),
    )
    span_rows = kv_key.shape[2]
    ctx_index = lax.axis_index("ctx")
    ctx_count = lax.axis_size("ctx")
    is_last = ctx_index == ctx_count - 1
    rim_from = span_rows - span_rows
    outgoing = jnp.stack(
        [
            jnp.stack([kv_key[0, 1, rim_from:], kv_value[0, 1, rim_from:]]),
            jnp.stack([kv_key[0, 0, rim_from:], kv_value[0, 0, rim_from:]]),
        ]
    )
    incoming = padded_2(outgoing, (("ctx", 0),), 1)
    previous = [incoming[0], jnp.where(is_last, outgoing[1], incoming[3])]
    run_begin = (
        lax.cummax(
            jnp.where(doc_start == 1, jnp.arange(doc_start.shape[0], dtype=jnp.int32), 0), axis=0
        )
        * BLK
    )
    blocks = span_rows // BLK
    span_results = []
    for span_slot in range(2):
        span_id = ctx_index if span_slot == 0 else 2 * ctx_count - 1 - ctx_index
        span_start = span_id * span_rows
        doc_begins = lax.dynamic_slice_in_dim(run_begin, span_id * blocks, blocks)
        keys_ext = jnp.concatenate([previous[span_slot][0], kv_key[0, span_slot]], axis=0)
        values_ext = jnp.concatenate([previous[span_slot][1], kv_value[0, span_slot]], axis=0)
        span_results.append(
            span_grads(
                query[0, span_slot],
                d_out[0, span_slot],
                keys_ext,
                values_ext,
                doc_begins,
                span_start,
                span_rows,
            )
        )
    partials = jnp.stack(
        [
            jnp.stack([span_results[0][1][:span_rows], span_results[0][2][:span_rows]]),
            jnp.stack([span_results[1][1][:span_rows], span_results[1][2][:span_rows]]),
        ]
    )
    returned = padded_2(partials.astype(jnp.bfloat16), (("ctx", 0),), 1).astype(partials.dtype)
    added_parts = [returned[3] + jnp.where(is_last, partials[1], 0.0), returned[0]]
    key_grads = []
    value_grads = []
    for span_slot in range(2):
        own_key = (
            span_results[span_slot][1][span_rows:].at[rim_from:].add(added_parts[span_slot][0])
        )
        own_value = (
            span_results[span_slot][2][span_rows:].at[rim_from:].add(added_parts[span_slot][1])
        )
        key_grads.append(own_key.astype(jnp.bfloat16))
        value_grads.append(own_value.astype(jnp.bfloat16))
    d_query = jnp.stack([span_results[0][0], span_results[1][0]])[None]
    key_layout = jnp.stack(key_grads)[None]
    value_layout = jnp.stack(value_grads)[None]
    d_key, d_value = (
        lax.all_to_all(key_layout, "head", split_axis=2, concat_axis=3, tiled=True),
        lax.all_to_all(value_layout, "head", split_axis=2, concat_axis=3, tiled=True),
    )
    return (d_query, d_key, d_value)


def solution(mesh):
    return jax.shard_map(
        per_device,
        mesh=mesh,
        in_specs=(
            P("ctx", None, None, "head"),
            P("ctx", None, "head", None),
            P("ctx", None, "head", None),
            P("ctx", None, None, "head"),
            P(),
        ),
        out_specs=(
            P("ctx", None, None, "head"),
            P("ctx", None, "head", None),
            P("ctx", None, "head", None),
        ),
        check_vma=False,
    )
```

profile of v0, /device:TPU:26, one launch (start us, length us, event | category | flops | bytes accessed | tf_op | source)
XLA Modules:
  0.0 143.1 jit_solution(6247647339542804097)
XLA Ops:
  0.6 1.8 %copy.44 = bf16[1,2,128,512]{2,1,0,3:T(2,128)(2,1)} copy(bf16[1,2,128,512]{3,2,1,0:T(8,128)(2,1)} %param.22) | data formatting | bytes 524288 | tf_op args[1]
  2.5 4.8 %all-to-all-start = ((bf16[1,2,128,512]{2,1,0,3:T(2,128)(2,1)}), bf16[1,2,128,512]{2,1,0,3:T(2,128)(2,1)S(1)}, u32[]{:S(2)}, u32[]{:S(2)}) async-start(bf16[1,2,128,512]{2,1,0,3:T(2,128)(2,1)} %copy.44), calls=%async_computation | async-start | bytes 524288 | tf_op jit(solution)/shard_map/all_to_all | solution.py:100
  8.6 1.8 %copy.46 = bf16[1,2,128,512]{2,1,0,3:T(2,128)(2,1)} copy(bf16[1,2,128,512]{3,2,1,0:T(8,128)(2,1)} %param.23) | data formatting | bytes 524288 | tf_op args[2]
  10.4 1.7 %slice_bitcast_fusion.1 = (bf16[64,8,8,128]{3,1,2,0:T(8,128)(2,1)S(1)}, bf16[64,8,8,128]{3,1,2,0:T(8,128)(2,1)S(1)}) fusion(bf16[1,2,512,1024]{3,2,1,0:T(8,128)(2,1)} %param.21), kind=kLoop, calls=%fused_computation.56 | loop fusion | bytes 4194304
  12.1 4.6 %slice_bitcast_fusion.3 = (bf16[64,8,8,128]{3,1,2,0:T(8,128)(2,1)}, f32[64,8,8,128]{3,1,2,0:T(8,128)}, f32[64,8,8,128]{3,1,2,0:T(8,128)}, bf16[64,8,8,128]{3,1,2,0:T(8,128)(2,1)}) fusion(bf16[1,2,512,1024]{3,2,1,0:T(8,128)(2,1)} %param.24), kind=kLoop, calls=%fused_computation.68 | loop fusion | flops 1048576 | bytes 8388608
  16.9 4.8 %all-to-all-start.1 = ((bf16[1,2,128,512]{2,1,0,3:T(2,128)(2,1)}), bf16[1,2,128,512]{2,1,0,3:T(2,128)(2,1)S(1)}, u32[]{:S(2)}, u32[]{:S(2)}) async-start(bf16[1,2,128,512]{2,1,0,3:T(2,128)(2,1)} %copy.46), calls=%async_computation.1 | async-start | bytes 524288 | tf_op jit(solution)/shard_map/all_to_all | solution.py:101
  22.5 4.3 %all-to-all-done.1 = bf16[1,2,128,512]{2,1,0,3:T(2,128)(2,1)S(1)} async-done(((bf16[1,2,128,512]{2,1,0,3:T(2,128)(2,1)}), bf16[1,2,128,512]{2,1,0,3:T(2,128)(2,1)S(1)}, u32[]{:S(2)}, u32[]{:S(2)}) %all-to-all-start.1) | async-done | bytes 262176 | tf_op jit(solution)/shard_map/all_to_all | solution.py:101
  27.1 1.0 fusion.102
  28.8 5.4 %collective-permute-start.1 = (bf16[1,2,512,128]{3,2,1,0:T(8,128)(2,1)}, bf16[1,2,512,128]{3,2,1,0:T(8,128)(2,1)}, u32[]{:S(2)}, u32[]{:S(2)}) collective-permute-start(bf16[1,2,512,128]{3,2,1,0:T(8,128)(2,1)} %maximum_bitcast_fusion.1), channel_id=1, source_target_pairs={{4,0},{8,4},{12,8},{16,12},{20,16},{24,20},{28,24},{32,28},{36,32}... | collective-permute-start | bytes 786440 | tf_op jit(solution)/shard_map/ppermute | solution.py:21
  34.8 2.5 %copy.98 = bf16[64,8,8,128]{3,2,1,0:T(8,128)(2,1)} copy(bf16[64,8,8,128]{3,1,2,0:T(8,128)(2,1)} %get-tuple-element.83) | data formatting | bytes 2097152
  37.3 1.5 %copy.101 = bf16[64,8,8,128]{3,2,1,0:T(8,128)(2,1)S(1)} copy(bf16[64,8,8,128]{3,1,2,0:T(8,128)(2,1)} %get-tuple-element.86) | data formatting | bytes 2097152
  38.8 3.4 %copy.99 = f32[64,8,8,128]{3,2,1,0:T(8,128)} copy(f32[64,8,8,128]{3,1,2,0:T(8,128)} %get-tuple-element.84) | data formatting | bytes 4194304
  42.2 2.9 %copy.52 = f32[4,128,1,8,128]{1,4,3,0,2:T(8,128)} copy(f32[4,128,1,8,128]{4,3,2,1,0:T(8,128)} %bitcast.414) | data formatting | bytes 4194304 | tf_op jit(solution)/shard_map/convert_element_type | solution.py:75
  45.1 3.4 %copy.102 = f32[64,8,8,128]{3,2,1,0:T(8,128)} copy(f32[64,8,8,128]{3,1,2,0:T(8,128)} %get-tuple-element.85) | data formatting | bytes 4194304
  48.5 2.9 %copy.60 = f32[4,128,1,8,128]{1,4,3,0,2:T(8,128)} copy(f32[4,128,1,8,128]{4,3,2,1,0:T(8,128)} %bitcast.415) | data formatting | bytes 4194304 | tf_op jit(solution)/shard_map/convert_element_type | solution.py:75
  51.4 2.2 %broadcast_and_fusion.1 = (pred[4,128,640]{1,2,0:T(8,128)(4,1)S(1)}, pred[4,128,640]{1,2,0:T(8,128)(4,1)S(1)}) fusion(pred[4,640]{1,0:T(4,128)(4,1)S(1)} %get-tuple-element.162, pred[128,640]{0,1:T(8,128)(4,1)} %iota_compare_fusion, pred[4,640]{1,0:T(4,128)(4,1)S(1)} %get-tuple-element.161), kind=kLoop, calls=%fused_computation.78 | loop fusion | flops 655360 | bytes 742400 | tf_op jit(solution)/shard_map/and | solution.py:62
  53.6 1.8 %fusion.81 = (bf16[1,2,512,128]{3,2,1,0:T(8,128)(2,1)}, bf16[2,512,128]{2,1,0:T(8,128)(2,1)S(1)}) fusion(bf16[1,512,128]{2,1,0:T(8,128)(2,1)} %get-tuple-element.159, bf16[1,512,128]{2,1,0:T(8,128)(2,1)} %get-tuple-element.114, bf16[1,2,512,128]{3,2,1,0:T(8,128)(2,1)} %collective-permute-done.1, pred[]{:T(512)S(6)} %eq.11), kind=kLoop, calls=%fused_computation.125 | loop fusion | flops 262144 | bytes 1048577 | tf_op jit(solution)/shard_map/stack | solution.py:108
  55.4 2.1 %collective-permute-start = (bf16[1,2,512,128]{3,2,1,0:T(8,128)(2,1)}, bf16[1,2,512,128]{3,2,1,0:T(8,128)(2,1)}, u32[]{:S(2)}, u32[]{:S(2)}) collective-permute-start(bf16[1,2,512,128]{3,2,1,0:T(8,128)(2,1)} %get-tuple-element.135), channel_id=1, source_target_pairs={{0,4},{4,8},{8,12},{12,16},{16,20},{20,24},{24,28},{28,32},{32,36}... | collective-permute-start | bytes 786440 | tf_op jit(solution)/shard_map/ppermute | solution.py:19
  58.9 1.6 %fusion.6 = (f32[4,8,128]{2,1,0:T(8,128)S(1)}, f32[4,640,128,8]{2,1,3,0:T(8,128)S(1)}) fusion(pred[4,128,640]{1,2,0:T(8,128)(4,1)S(1)} %get-tuple-element.148, bf16[4,128,8,128]{3,2,1,0:T(8,128)(2,1)S(1)} %bitcast.412, bf16[4,640,1,128]{3,1,0,2:T(8,128)(2,1)S(1)} %constant_dynamic-update-slice_fusion.10), kind=kOutput, calls=%fused_computation.10 | convolution fusion | flops 678948864 | bytes 12533760 | tf_op jit(solution)/shard_map/btgjd,bkgd->bgjtk/dot_general | solution.py:65
  60.5 2.4 %fusion.15 = f32[4,8,128]{2,1,0:T(8,128)S(1)} fusion(f32[4,640,128,8]{2,1,3,0:T(8,128)S(1)} %get-tuple-element.152, f32[4,8,128]{2,1,0:T(8,128)S(1)} %get-tuple-element.151, pred[4,128,640]{1,2,0:T(8,128)(4,1)S(1)} %get-tuple-element.148), kind=kLoop, calls=%fused_computation.21 | loop fusion | flops 10481664 | bytes 10846208 | tf_op jit(solution)/shard_map/reduce_sum | solution.py:70
  62.9 3.1 %fusion.41 = f32[4,640,1,128]{3,1,0,2:T(8,128)S(1)} fusion(bf16[4,128,8,128]{3,2,1,0:T(8,128)(2,1)S(1)} %bitcast.439, f32[4,8,128]{2,1,0:T(8,128)S(1)} %fusion.15, f32[4,8,128]{2,1,0:T(8,128)S(1)} %get-tuple-element.151, f32[4,640,128,8]{2,1,3,0:T(8,128)S(1)} %get-tuple-element.152, pred[4,128,640]{1,2,0:T(8,128)(4,1)S(1)} %get-tuple-element.148), kind=kOutput, calls=%fused_computation.50 | convolution fusion | flops 684195840 | bytes 13205504 | tf_op jit(solution)/shard_map/bgjtk,btgjd->bkgd/dot_general | solution.py:88
  66.1 3.2 %fusion.29 = f32[4,128,8]{1,2,0:T(8,128)S(1)} fusion(f32[4,128,1,8,128]{1,4,3,0,2:T(8,128)S(1)} %copy-done.6, bf16[4,640,1,128]{3,1,0,2:T(8,128)(2,1)S(1)} %constant_dynamic-update-slice_fusion.15, f32[4,8,128]{2,1,0:T(8,128)S(1)} %fusion.15, f32[4,8,128]{2,1,0:T(8,128)S(1)} %get-tuple-element.151, f32[4,640,128,8]{2,1,3,0:T(8,128)S(1)} %get-tuple-element.152, ...), kind=kOutput, calls=%fused_computation.37 | convolution fusion | flops 686288896 | bytes 13615104 | tf_op jit(solution)/shard_map/bgjtk,bkgd->btgjd/dot_general | solution.py:72
  69.2 4.2 %fusion.17 = bf16[4,8,128,640]{2,3,1,0:T(8,128)(2,1)S(1)} fusion(f32[4,8,128]{2,1,0:T(8,128)S(1)} %bitcast.468, f32[4,8,128]{2,1,0:T(8,128)S(1)} %fusion.15, f32[4,8,128]{2,1,0:T(8,128)S(1)} %get-tuple-element.151, f32[4,640,128,8]{2,1,3,0:T(8,128)S(1)} %get-tuple-element.152, pred[4,128,640]{1,2,0:T(8,128)(4,1)S(1)} %get-tuple-element.148, ...), kind=kOutput, calls=%fused_computation.23 | convolution fusion | flops 692060160 | bytes 17809408 | tf_op jit(solution)/shard_map/btgjd,bkgd->bgjtk/dot_general | solution.py:76
  73.6 1.5 %convolution_bitcast_fusion = f32[4,640,1,128]{3,1,0,2:T(8,128)S(1)} fusion(bf16[4,8,128,640]{2,3,1,0:T(8,128)(2,1)S(1)} %fusion.17, bf16[4,128,8,128]{3,2,1,0:T(8,128)(2,1)S(1)} %bitcast.413), kind=kOutput, calls=%fused_computation.47 | convolution fusion | flops 671088640 | bytes 7602176 | tf_op jit(solution)/shard_map/bgjtk,btgjd->bkgd/dot_general | solution.py:85
  76.2 2.1 %collective-permute-start.2 = (bf16[1,2,512,128]{3,2,1,0:T(8,128)(2,1)S(1)}, bf16[1,2,512,128]{3,2,1,0:T(8,128)(2,1)S(1)}, u32[]{:S(2)}, u32[]{:S(2)}) collective-permute-start(bf16[1,2,512,128]{3,2,1,0:T(8,128)(2,1)S(1)} %fusion.76), channel_id=1, source_target_pairs={{0,4},{4,8},{8,12},{12,16},{16,20},{20,24},{24,28},{28,32},{32,36}... | collective-permute-start | bytes 786440 | tf_op jit(solution)/shard_map/ppermute | solution.py:19
  78.4 1.0 slice_bitcast_fusion.12
  79.9 1.6 %fusion.9 = (f32[4,8,128]{2,1,0:T(8,128)S(1)}, f32[4,640,128,8]{2,1,3,0:T(8,128)S(1)}) fusion(pred[4,128,640]{1,2,0:T(8,128)(4,1)S(1)} %get-tuple-element.147, bf16[4,128,8,128]{3,2,1,0:T(8,128)(2,1)S(1)} %bitcast.410, bf16[4,640,1,128]{3,1,0,2:T(8,128)(2,1)S(1)} %constant_dynamic-update-slice_fusion), kind=kOutput, calls=%fused_computation.15 | convolution fusion | flops 678948864 | bytes 12533760 | tf_op jit(solution)/shard_map/btgjd,bkgd->bgjtk/dot_general | solution.py:65
  81.5 2.4 %fusion.13 = f32[4,8,128]{2,1,0:T(8,128)S(1)} fusion(f32[4,640,128,8]{2,1,3,0:T(8,128)S(1)} %get-tuple-element.154, f32[4,8,128]{2,1,0:T(8,128)S(1)} %get-tuple-element.153, pred[4,128,640]{1,2,0:T(8,128)(4,1)S(1)} %get-tuple-element.147), kind=kLoop, calls=%fused_computation.19 | loop fusion | flops 10481664 | bytes 10846208 | tf_op jit(solution)/shard_map/reduce_sum | solution.py:70
  83.9 4.2 %fusion.38 = f32[4,640,1,128]{3,1,0,2:T(8,128)S(1)} fusion(bf16[4,128,8,128]{3,2,1,0:T(8,128)(2,1)} %bitcast.437, f32[4,8,128]{2,1,0:T(8,128)S(1)} %fusion.13, f32[4,8,128]{2,1,0:T(8,128)S(1)} %get-tuple-element.153, f32[4,640,128,8]{2,1,3,0:T(8,128)S(1)} %get-tuple-element.154, pred[4,128,640]{1,2,0:T(8,128)(4,1)S(1)} %get-tuple-element.147), kind=kOutput, calls=%fused_computation.49 | convolution fusion | flops 684195840 | bytes 13205504 | tf_op jit(solution)/shard_map/bgjtk,btgjd->bkgd/dot_general | solution.py:88
  88.2 4.4 %fusion.31 = f32[4,128,8]{1,2,0:T(8,128)S(1)} fusion(f32[4,128,1,8,128]{1,4,3,0,2:T(8,128)S(1)} %copy-done.5, bf16[4,640,1,128]{3,1,0,2:T(8,128)(2,1)} %copy-done.14, f32[4,8,128]{2,1,0:T(8,128)S(1)} %fusion.13, f32[4,8,128]{2,1,0:T(8,128)S(1)} %get-tuple-element.153, f32[4,640,128,8]{2,1,3,0:T(8,128)S(1)} %get-tuple-element.154, ...), kind=kOutput, calls=%fused_computation.40 | convolution fusion | flops 686288896 | bytes 13615104 | tf_op jit(solution)/shard_map/bgjtk,bkgd->btgjd/dot_general | solution.py:72
  92.6 4.2 %fusion.16 = bf16[4,8,128,640]{2,3,1,0:T(8,128)(2,1)S(1)} fusion(f32[4,8,128]{2,1,0:T(8,128)S(1)} %bitcast.469, f32[4,8,128]{2,1,0:T(8,128)S(1)} %fusion.13, f32[4,8,128]{2,1,0:T(8,128)S(1)} %get-tuple-element.153, f32[4,640,128,8]{2,1,3,0:T(8,128)S(1)} %get-tuple-element.154, pred[4,128,640]{1,2,0:T(8,128)(4,1)S(1)} %get-tuple-element.147, ...), kind=kOutput, calls=%fused_computation.22 | convolution fusion | flops 692060160 | bytes 17809408 | tf_op jit(solution)/shard_map/btgjd,bkgd->bgjtk/dot_general | solution.py:76
  97.0 2.1 %copy-done = bf16[4,8,128,640]{2,3,1,0:T(8,128)(2,1)} copy-done((bf16[4,8,128,640]{2,3,1,0:T(8,128)(2,1)}, bf16[4,8,128,640]{2,3,1,0:T(8,128)(2,1)S(1)}, u32[]{:S(2)}) %copy-start) | copy-done | bytes 5242904
  99.1 1.5 %convolution_bitcast_fusion.1 = f32[4,640,1,128]{3,1,0,2:T(8,128)S(1)} fusion(bf16[4,8,128,640]{2,3,1,0:T(8,128)(2,1)S(1)} %fusion.16, bf16[4,128,8,128]{3,2,1,0:T(8,128)(2,1)S(1)} %bitcast.411), kind=kOutput, calls=%fused_computation.48 | convolution fusion | flops 671088640 | bytes 7602176 | tf_op jit(solution)/shard_map/bgjtk,btgjd->bkgd/dot_general | solution.py:85
  101.7 6.0 %collective-permute-start.3 = (bf16[1,2,512,128]{3,2,1,0:T(8,128)(2,1)S(1)}, bf16[1,2,512,128]{3,2,1,0:T(8,128)(2,1)S(1)}, u32[]{:S(2)}, u32[]{:S(2)}) collective-permute-start(bf16[1,2,512,128]{3,2,1,0:T(8,128)(2,1)S(1)} %maximum_bitcast_fusion.2), channel_id=1, source_target_pairs={{4,0},{8,4},{12,8},{16,12},{20,16},{24,20},{28,24},{32,28},{36,32}... | collective-permute-start | bytes 786440 | tf_op jit(solution)/shard_map/ppermute | solution.py:21
  107.7 2.0 %fusion.45 = bf16[4,128,1,8,128]{1,4,3,0,2:T(8,128)(2,1)} fusion(bf16[4,8,128,640]{2,3,1,0:T(8,128)(2,1)S(1)} %fusion.17, bf16[4,640,1,128]{3,1,0,2:T(8,128)(2,1)S(1)} %constant_dynamic-update-slice_fusion.10), kind=kOutput, calls=%fused_computation.52 | convolution fusion | flops 671612928 | bytes 6946816 | tf_op jit(solution)/shard_map/bgjtk,bkgd->btgjd/dot_general | solution.py:82
  109.7 1.7 %copy.63 = bf16[4,128,1,8,128]{4,3,1,0,2:T(8,128)(2,1)S(1)} copy(bf16[4,128,1,8,128]{1,4,3,0,2:T(8,128)(2,1)} %fusion.45) | data formatting | bytes 2097152 | tf_op jit(solution)/shard_map/convert_element_type | solution.py:84
  111.4 1.3 stack_reshape.7
  112.8 1.2 fusion.79
  113.9 1.0 fusion.78
  115.9 4.8 %all-to-all-start.3 = ((bf16[1,2,512,128]{3,1,0,2:T(2,128)(2,1)}), bf16[1,2,512,128]{3,1,0,2:T(2,128)(2,1)S(1)}, u32[]{:S(2)}, u32[]{:S(2)}) async-start(bf16[1,2,512,128]{3,1,0,2:T(2,128)(2,1)} %copy.71), calls=%async_computation.3 | async-start | bytes 524288 | tf_op jit(solution)/shard_map/all_to_all | solution.py:165
  120.8 1.2 add_convert_fusion
  122.2 1.3 maximum_bitcast_fusion.3
  123.5 2.5 %all-to-all-done.3 = bf16[1,2,512,128]{3,1,0,2:T(2,128)(2,1)S(1)} async-done(((bf16[1,2,512,128]{3,1,0,2:T(2,128)(2,1)}), bf16[1,2,512,128]{3,1,0,2:T(2,128)(2,1)S(1)}, u32[]{:S(2)}, u32[]{:S(2)}) %all-to-all-start.3) | async-done | bytes 262176 | tf_op jit(solution)/shard_map/all_to_all | solution.py:165
  126.0 4.8 %all-to-all-start.2 = ((bf16[1,2,512,128]{3,1,0,2:T(2,128)(2,1)}), bf16[1,2,512,128]{3,1,0,2:T(2,128)(2,1)S(1)}, u32[]{:S(2)}, u32[]{:S(2)}) async-start(bf16[1,2,512,128]{3,1,0,2:T(2,128)(2,1)} %maximum_bitcast_fusion.3), calls=%async_computation.2 | async-start | bytes 524288 | tf_op jit(solution)/shard_map/all_to_all | solution.py:164
  130.8 4.5 %fusion.44 = bf16[4,128,1,8,128]{1,4,3,0,2:T(8,128)(2,1)} fusion(bf16[4,8,128,640]{2,3,1,0:T(8,128)(2,1)} %copy-done, bf16[4,640,1,128]{3,1,0,2:T(8,128)(2,1)S(1)} %constant_dynamic-update-slice_fusion), kind=kOutput, calls=%fused_computation.51 | convolution fusion | flops 671612928 | bytes 6946816 | tf_op jit(solution)/shard_map/bgjtk,bkgd->btgjd/dot_general | solution.py:82
  135.4 1.7 %copy.55 = bf16[4,128,1,8,128]{4,3,1,0,2:T(8,128)(2,1)S(1)} copy(bf16[4,128,1,8,128]{1,4,3,0,2:T(8,128)(2,1)} %fusion.44) | data formatting | bytes 2097152 | tf_op jit(solution)/shard_map/convert_element_type | solution.py:84
  137.0 1.3 stack_reshape.6
  138.3 2.7 %maximum_bitcast_fusion = bf16[1,2,512,1024]{3,2,1,0:T(8,128)(2,1)} fusion(bf16[1,512,1024]{2,1,0:T(8,128)(2,1)S(1)} %copy-done.1, bf16[1,512,1024]{2,1,0:T(8,128)(2,1)} %stack_reshape.6), kind=kLoop, calls=%fused_computation.34 | loop fusion | flops 1048576 | bytes 4194304 | tf_op jit(solution)/shard_map/broadcast_in_dim | solution.py:160
  (102 shorter events, 11.1 us)
Async XLA Ops:
  2.5 14.4 %all-to-all-start = ((bf16[1,2,128,512]{2,1,0,3:T(2,128)(2,1)}), bf16[1,2,128,512]{2,1,0,3:T(2,128)(2,1)S(1)}, u32[]{:S(2)}, u32[]{:S(2)}) async-start(bf16[1,2,128,512]{2,1,0,3:T(2,128)(2,1)} %copy.44), calls=%async_computation | async-start | bytes 524288 | tf_op jit(solution)/shard_map/all_to_all | solution.py:100
  16.9 10.0 %all-to-all-start.1 = ((bf16[1,2,128,512]{2,1,0,3:T(2,128)(2,1)}), bf16[1,2,128,512]{2,1,0,3:T(2,128)(2,1)S(1)}, u32[]{:S(2)}, u32[]{:S(2)}) async-start(bf16[1,2,128,512]{2,1,0,3:T(2,128)(2,1)} %copy.46), calls=%async_computation.1 | async-start | bytes 524288 | tf_op jit(solution)/shard_map/all_to_all | solution.py:101
  28.8 24.8 %collective-permute-start.1 = (bf16[1,2,512,128]{3,2,1,0:T(8,128)(2,1)}, bf16[1,2,512,128]{3,2,1,0:T(8,128)(2,1)}, u32[]{:S(2)}, u32[]{:S(2)}) collective-permute-start(bf16[1,2,512,128]{3,2,1,0:T(8,128)(2,1)} %maximum_bitcast_fusion.1), channel_id=1, source_target_pairs={{4,0},{8,4},{12,8},{16,12},{20,16},{24,20},{28,24},{32,28},{36,32}... | collective-permute-start | bytes 786440 | tf_op jit(solution)/shard_map/ppermute | solution.py:21
  55.4 23.0 %collective-permute-start = (bf16[1,2,512,128]{3,2,1,0:T(8,128)(2,1)}, bf16[1,2,512,128]{3,2,1,0:T(8,128)(2,1)}, u32[]{:S(2)}, u32[]{:S(2)}) collective-permute-start(bf16[1,2,512,128]{3,2,1,0:T(8,128)(2,1)} %get-tuple-element.135), channel_id=1, source_target_pairs={{0,4},{4,8},{8,12},{12,16},{16,20},{20,24},{24,28},{28,32},{32,36}... | collective-permute-start | bytes 786440 | tf_op jit(solution)/shard_map/ppermute | solution.py:19
  62.9 3.1 %copy-start.6 = (f32[4,128,1,8,128]{1,4,3,0,2:T(8,128)S(1)}, f32[4,128,1,8,128]{1,4,3,0,2:T(8,128)}, u32[]{:S(2)}) copy-start(f32[4,128,1,8,128]{1,4,3,0,2:T(8,128)} %copy.60) | copy-start | bytes 6291460
  73.5 6.0 %copy-start.11 = (bf16[512,128]{1,0:T(8,128)(2,1)S(1)}, bf16[512,128]{1,0:T(8,128)(2,1)}, u32[]{:S(2)}) copy-start(bf16[512,128]{1,0:T(8,128)(2,1)} %get-tuple-element.115) | copy-start | bytes 393220
  73.5 6.1 %copy-start.10 = (bf16[512,128]{1,0:T(8,128)(2,1)S(1)}, bf16[512,128]{1,0:T(8,128)(2,1)}, u32[]{:S(2)}) copy-start(bf16[512,128]{1,0:T(8,128)(2,1)} %get-tuple-element.158) | copy-start | bytes 393220
  73.6 6.1 %copy-start.13 = (bf16[1,1,512,128]{3,2,1,0:T(8,128)(2,1)S(1)}, bf16[1,1,512,128]{3,2,1,0:T(8,128)(2,1)}, u32[]{:S(2)}) copy-start(bf16[1,1,512,128]{3,2,1,0:T(8,128)(2,1)} %get-tuple-element.160) | copy-start | bytes 393220
  73.6 6.2 %copy-start.12 = (bf16[1,1,512,128]{3,2,1,0:T(8,128)(2,1)S(1)}, bf16[1,1,512,128]{3,2,1,0:T(8,128)(2,1)}, u32[]{:S(2)}) copy-start(bf16[1,1,512,128]{3,2,1,0:T(8,128)(2,1)} %get-tuple-element.113) | copy-start | bytes 393220
  76.1 5.4 %copy-start.2 = (f32[1,512,128]{2,1,0:T(8,128)}, f32[1,512,128]{2,1,0:T(8,128)S(1)}, u32[]{:S(2)}) copy-start(f32[1,512,128]{2,1,0:T(8,128)S(1)} %get-tuple-element.111) | copy-start | bytes 786436
  76.2 5.4 %copy-start.4 = (f32[1024,1,128]{2,0,1:T(8,128)}, f32[1024,1,128]{2,0,1:T(8,128)S(1)}, u32[]{:S(2)}) copy-start(f32[1024,1,128]{2,0,1:T(8,128)S(1)} %pad_add_fusion.1) | copy-start | bytes 1572868
  76.2 36.5 %collective-permute-start.2 = (bf16[1,2,512,128]{3,2,1,0:T(8,128)(2,1)S(1)}, bf16[1,2,512,128]{3,2,1,0:T(8,128)(2,1)S(1)}, u32[]{:S(2)}, u32[]{:S(2)}) collective-permute-start(bf16[1,2,512,128]{3,2,1,0:T(8,128)(2,1)S(1)} %fusion.76), channel_id=1, source_target_pairs={{0,4},{4,8},{8,12},{12,16},{16,20},{20,24},{24,28},{28,32},{32,36}... | collective-permute-start | bytes 786440 | tf_op jit(solution)/shard_map/ppermute | solution.py:19
  79.7 4.2 %copy-start.14 = (bf16[4,640,1,128]{3,1,0,2:T(8,128)(2,1)}, bf16[4,640,1,128]{3,1,0,2:T(8,128)(2,1)S(1)}, u32[]{:S(2)}) copy-start(bf16[4,640,1,128]{3,1,0,2:T(8,128)(2,1)S(1)} %constant_dynamic-update-slice_fusion.5) | copy-start | bytes 1966084
  83.9 4.2 %copy-start.5 = (f32[4,128,1,8,128]{1,4,3,0,2:T(8,128)S(1)}, f32[4,128,1,8,128]{1,4,3,0,2:T(8,128)}, u32[]{:S(2)}) copy-start(f32[4,128,1,8,128]{1,4,3,0,2:T(8,128)} %copy.52) | copy-start | bytes 6291460
  88.2 4.4 %copy-start.9 = (bf16[64,8,8,128]{3,2,1,0:T(8,128)(2,1)S(1)}, bf16[64,8,8,128]{3,2,1,0:T(8,128)(2,1)}, u32[]{:S(2)}) copy-start(bf16[64,8,8,128]{3,2,1,0:T(8,128)(2,1)} %copy.98) | copy-start | bytes 3145732
  88.2 4.4 %copy-start.15 = (bf16[4,640,1,128]{3,1,0,2:T(8,128)(2,1)S(1)}, bf16[4,640,1,128]{3,1,0,2:T(8,128)(2,1)}, u32[]{:S(2)}) copy-start(bf16[4,640,1,128]{3,1,0,2:T(8,128)(2,1)} %copy-done.14) | copy-start | bytes 1966084
  96.8 2.3 %copy-start = (bf16[4,8,128,640]{2,3,1,0:T(8,128)(2,1)}, bf16[4,8,128,640]{2,3,1,0:T(8,128)(2,1)S(1)}, u32[]{:S(2)}) copy-start(bf16[4,8,128,640]{2,3,1,0:T(8,128)(2,1)S(1)} %fusion.16) | copy-start | bytes 15728644
  97.0 10.7 %copy-start.7 = (f32[1024,1,128]{2,0,1:T(8,128)}, f32[1024,1,128]{2,0,1:T(8,128)S(1)}, u32[]{:S(2)}) copy-start(f32[1024,1,128]{2,0,1:T(8,128)S(1)} %pad_add_fusion) | copy-start | bytes 1572868
  100.7 12.0 %copy-start.3 = (f32[1,512,128]{2,1,0:T(8,128)S(1)}, f32[1,512,128]{2,1,0:T(8,128)}, u32[]{:S(2)}) copy-start(f32[1,512,128]{2,1,0:T(8,128)} %copy-done.2) | copy-start | bytes 786436
  100.9 0.8 copy-start.8
  101.7 11.0 %collective-permute-start.3 = (bf16[1,2,512,128]{3,2,1,0:T(8,128)(2,1)S(1)}, bf16[1,2,512,128]{3,2,1,0:T(8,128)(2,1)S(1)}, u32[]{:S(2)}, u32[]{:S(2)}) collective-permute-start(bf16[1,2,512,128]{3,2,1,0:T(8,128)(2,1)S(1)} %maximum_bitcast_fusion.2), channel_id=1, source_target_pairs={{4,0},{8,4},{12,8},{16,12},{20,16},{24,20},{28,24},{32,28},{36,32}... | collective-permute-start | bytes 786440 | tf_op jit(solution)/shard_map/ppermute | solution.py:21
  112.7 25.6 %copy-start.1 = (bf16[1,512,1024]{2,1,0:T(8,128)(2,1)S(1)}, bf16[1,512,1024]{2,1,0:T(8,128)(2,1)}, u32[]{:S(2)}) copy-start(bf16[1,512,1024]{2,1,0:T(8,128)(2,1)} %stack_reshape.7) | copy-start | bytes 3145732
  115.9 10.1 %all-to-all-start.3 = ((bf16[1,2,512,128]{3,1,0,2:T(2,128)(2,1)}), bf16[1,2,512,128]{3,1,0,2:T(2,128)(2,1)S(1)}, u32[]{:S(2)}, u32[]{:S(2)}) async-start(bf16[1,2,512,128]{3,1,0,2:T(2,128)(2,1)} %copy.71), calls=%async_computation.3 | async-start | bytes 524288 | tf_op jit(solution)/shard_map/all_to_all | solution.py:165
  126.0 16.1 %all-to-all-start.2 = ((bf16[1,2,512,128]{3,1,0,2:T(2,128)(2,1)}), bf16[1,2,512,128]{3,1,0,2:T(2,128)(2,1)S(1)}, u32[]{:S(2)}, u32[]{:S(2)}) async-start(bf16[1,2,512,128]{3,1,0,2:T(2,128)(2,1)} %maximum_bitcast_fusion.3), calls=%async_computation.2 | async-start | bytes 524288 | tf_op jit(solution)/shard_map/all_to_all | solution.py:164
where the time goes:
time: 144 us; the launch traced here: 143 us
  local copies, waits for them, and re-layouts  39.7 us (28%)
  matrix products  36.2 us (25%)
  starting transfers between devices  34.9 us (24%)
  other arithmetic  24.1 us (17%)
  waiting for transfers between devices  6.8 us (5%)
    unnamed x57, local copies, waits for them, and re-layouts  19.9 us
    ppermute x2, starting transfers between devices, padded_2(): lax.ppermute(head, axis, [((i + 1) % count, i) for i in range(ends)])  11.4 us
    dot_general x2, matrix products, span_grads(): jnp.einsum('btgjd,bkgd->bgjtk', do_blocks, v_windows, preferred_element_t...  8.42 us
    dot_general x2, matrix products, span_grads(): jnp.einsum('bgjtk,bkgd->btgjd', probs_b, v_windows, preferred_element_typ...  7.54 us
    dot_general x2, matrix products, span_grads(): jnp.einsum('bgjtk,btgjd->bkgd', probs_b, do_blocks, preferred_element_typ...  7.32 us
    dot_general x2, matrix products, span_grads(): jnp.einsum('bgjtk,bkgd->btgjd', dscores, k_windows, preferred_element_typ...  6.55 us
    convert_element_type x2, local copies, waits for them, and re-layouts, span_grads(): do_blocks.astype(jnp.float32) * outputs.astype(jnp.float32)  5.78 us
    all_to_all x1, starting transfers between devices, per_device(): lax.all_to_all(value_layout, 'head', split_axis=2, concat_axis=3, tiled=T...  4.84 us
  transfers between devices with their start and end apart: 8, of which 2 were waited for; matrix products, arithmetic and copies ran while one was open for 60% of the time, Pallas kernels for 0%

commit v1 on v0

--- a/solution.py
+++ b/solution.py
@@ -6,6 +6,28 @@
 HD = 128
 BLK = 128
 GROUP = 8
+
+
+def split_up(array, dim, devices):
+    before, after = (array.shape[:dim], array.shape[dim + 1 :])
+    return jnp.moveaxis(array.reshape(*before, devices, -1, *after), dim, 0)
+
+
+def in_order(pieces, dim):
+    pieces = jnp.moveaxis(pieces, 0, dim)
+    shape = pieces.shape
+    return pieces.reshape(*shape[:dim], shape[dim] * shape[dim + 1], *shape[dim + 2 :])
+
+
+def pairwise_exchange(array, axis, split_dim, concat_dim):
+    size, index = (lax.axis_size(axis), lax.axis_index(axis))
+    parts = split_up(array, split_dim, size)
+    outs = [parts[index]]
+    for step in range(1, size):
+        sent = parts[index ^ step]
+        outs.append(lax.ppermute(sent, axis, [(i, i ^ step) for i in range(size)]))
+    parts = jnp.stack(outs)[index ^ jnp.arange(size)]
+    return in_order(parts, concat_dim)
 
 
 def padded_2(cells, sides, width):
@@ -97,7 +119,7 @@
 
 def per_device(query, key, value, d_out, doc_start):
     kv_key, kv_value = (
-        lax.all_to_all(key, "head", split_axis=3, concat_axis=2, tiled=True),
+        pairwise_exchange(key, "head", 3, 2),
         lax.all_to_all(value, "head", split_axis=3, concat_axis=2, tiled=True),
     )
     span_rows = kv_key.shape[2]

time: 144 us -> 131 us (0.910)
  other arithmetic: 24.1 us -> 17.8 us
  local copies, waits for them, and re-layouts: 39.7 us -> 35.6 us
  waiting for transfers between devices: 6.8 us -> 3.88 us
    all_to_all x1 -> x0, starting transfers between devices: 4.82 us -> none  [per_device(): lax.all_to_all(key, 'head', split_axis=3, concat_axis=2, tiled=True)]
    all_to_all x1, waiting for transfers between devices: 4.33 us -> 0.01 us  [per_device(): lax.all_to_all(value, 'head', split_axis=3, concat_axis=2, tiled=True)]
    ppermute x2, waiting for transfers between devices: 0.01 us -> 3.86 us  [padded_2(): lax.ppermute(head, axis, [((i + 1) % count, i) for i in range(ends)])]
    ppermute x0 -> x3, starting transfers between devices: none -> 3.75 us  [pairwise_exchange(): outs.append(lax.ppermute(sent, axis, [(i, i ^ step) for i in range(size)]))]
    dot_general x2, matrix products: 6.55 us -> 9 us  [span_grads(): jnp.einsum('bgjtk,bkgd->btgjd', dscores, k_windows, preferred_element_typ...]
    all_to_all x1, waiting for transfers between devices: 2.45 us -> 0.01 us  [per_device(): lax.all_to_all(value_layout, 'head', split_axis=2, concat_axis=3, tiled=T...]
    unnamed x57 -> x53, local copies, waits for them, and re-layouts: 19.9 us -> 17.4 us
    convert_element_type x2, other arithmetic: 2.15 us -> 0.14 us  [per_device(): value_grads.append(own_value.astype(jnp.bfloat16))]
  transfers between devices with their start and end apart: 8 -> 10, of which waited for: 2 -> 1; matrix products, arithmetic and copies ran while one was open for 60% -> 63% of each run, Pallas kernels for 0% -> 0%
where the time goes in v1:
time: 131 us; the launch traced here: 130 us
  matrix products  36.3 us (28%)
  local copies, waits for them, and re-layouts  35.6 us (27%)
  starting transfers between devices  35.1 us (27%)
  other arithmetic  17.8 us (14%)
  waiting for transfers between devices  3.88 us (3%)
  between operations  1.51 us (1%)
    unnamed x53, local copies, waits for them, and re-layouts  17.4 us
    ppermute x2, starting transfers between devices, padded_2(): lax.ppermute(head, axis, [((i + 1) % count, i) for i in range(ends)])  11.7 us
    dot_general x2, matrix products, span_grads(): jnp.einsum('bgjtk,bkgd->btgjd', dscores, k_windows, preferred_element_typ...  9 us
    dot_general x2, matrix products, span_grads(): jnp.einsum('btgjd,bkgd->bgjtk', do_blocks, v_windows, preferred_element_t...  8.43 us
    dot_general x2, matrix products, span_grads(): jnp.einsum('bgjtk,bkgd->btgjd', probs_b, v_windows, preferred_element_typ...  6.34 us
    dot_general x2, matrix products, span_grads(): jnp.einsum('bgjtk,btgjd->bkgd', probs_b, do_blocks, preferred_element_typ...  6.25 us
    convert_element_type x2, local copies, waits for them, and re-layouts, span_grads(): do_blocks.astype(jnp.float32) * outputs.astype(jnp.float32)  5.84 us
    all_to_all x1, starting transfers between devices, per_device(): lax.all_to_all(value, 'head', split_axis=3, concat_axis=2, tiled=True)  5.77 us
  transfers between devices with their start and end apart: 10, of which 1 were waited for; matrix products, arithmetic and copies ran while one was open for 63% of the time, Pallas kernels for 0%

profile of v1, /device:TPU:26, one launch (start us, length us, event | category | flops | bytes accessed | tf_op | source)
XLA Modules:
  0.0 130.1 jit_solution(7569914711019329775)
XLA Ops:
  0.6 1.1 copy.73
  2.7 2.5 %collective-permute-start.1 = (bf16[1,2,128,128]{3,2,1,0:T(8,128)(2,1)S(1)}, bf16[1,2,128,128]{3,2,1,0:T(8,128)(2,1)S(1)}, u32[]{:S(2)}, u32[]{:S(2)}) collective-permute-start(bf16[1,2,128,128]{3,2,1,0:T(8,128)(2,1)S(1)} %bitcast.487), channel_id=1, source_target_pairs={{0,2},{1,3},{2,0},{3,1},{4,6},{5,7},{6,4},{7,5},{8,10},{9,11},{10,... | collective-permute-start | bytes 196616 | tf_op jit(solution)/shard_map/ppermute | solution.py:28
  5.3 0.6 collective-permute-start.2
  5.9 1.8 %copy.80 = bf16[1,2,128,512]{2,1,0,3:T(2,128)(2,1)} copy(bf16[1,2,128,512]{3,2,1,0:T(8,128)(2,1)} %param.23) | data formatting | bytes 524288 | tf_op args[2]
  7.8 5.8 %all-to-all-start = ((bf16[1,2,128,512]{2,1,0,3:T(2,128)(2,1)}), bf16[1,2,128,512]{2,1,0,3:T(2,128)(2,1)S(1)}, u32[]{:S(2)}, u32[]{:S(2)}) async-start(bf16[1,2,128,512]{2,1,0,3:T(2,128)(2,1)} %copy.80), calls=%async_computation | async-start | bytes 524288 | tf_op jit(solution)/shard_map/all_to_all | solution.py:123
  13.6 0.7 select_bitcast_fusion
  14.9 0.7 iota_compare_fusion
  15.7 1.7 %slice_bitcast_fusion.1 = (bf16[64,8,8,128]{3,1,2,0:T(8,128)(2,1)S(1)}, bf16[64,8,8,128]{3,1,2,0:T(8,128)(2,1)S(1)}) fusion(bf16[1,2,512,1024]{3,2,1,0:T(8,128)(2,1)} %param.21), kind=kLoop, calls=%fused_computation.57 | loop fusion | bytes 4194304
  17.4 4.7 %slice_bitcast_fusion.3 = (bf16[64,8,8,128]{3,1,2,0:T(8,128)(2,1)}, f32[64,8,8,128]{3,1,2,0:T(8,128)}, f32[64,8,8,128]{3,1,2,0:T(8,128)}, bf16[64,8,8,128]{3,1,2,0:T(8,128)(2,1)}) fusion(bf16[1,2,512,1024]{3,2,1,0:T(8,128)(2,1)} %param.24), kind=kLoop, calls=%fused_computation.69 | loop fusion | flops 1048576 | bytes 8388608
  23.1 1.0 fusion.105
  24.1 0.7 maximum_bitcast_fusion.2
  24.8 6.0 %collective-permute-start.4 = (bf16[1,2,512,128]{3,2,1,0:T(8,128)(2,1)}, bf16[1,2,512,128]{3,2,1,0:T(8,128)(2,1)}, u32[]{:S(2)}, u32[]{:S(2)}) collective-permute-start(bf16[1,2,512,128]{3,2,1,0:T(8,128)(2,1)} %maximum_bitcast_fusion.2), channel_id=1, source_target_pairs={{4,0},{8,4},{12,8},{16,12},{20,16},{24,20},{28,24},{32,28},{36,32}... | collective-permute-start | bytes 786440 | tf_op jit(solution)/shard_map/ppermute | solution.py:43
  31.4 2.6 %copy.133 = bf16[64,8,8,128]{3,2,1,0:T(8,128)(2,1)} copy(bf16[64,8,8,128]{3,1,2,0:T(8,128)(2,1)} %get-tuple-element.83) | data formatting | bytes 2097152
  34.0 2.5 %copy.136 = bf16[64,8,8,128]{3,2,1,0:T(8,128)(2,1)} copy(bf16[64,8,8,128]{3,1,2,0:T(8,128)(2,1)} %get-tuple-element.86) | data formatting | bytes 2097152
  36.6 3.4 %copy.134 = f32[64,8,8,128]{3,2,1,0:T(8,128)} copy(f32[64,8,8,128]{3,1,2,0:T(8,128)} %get-tuple-element.84) | data formatting | bytes 4194304
  40.0 2.9 %copy.86 = f32[4,128,1,8,128]{1,4,3,0,2:T(8,128)} copy(f32[4,128,1,8,128]{4,3,2,1,0:T(8,128)} %bitcast.433) | data formatting | bytes 4194304 | tf_op jit(solution)/shard_map/convert_element_type | solution.py:97
  42.9 3.4 %copy.137 = f32[64,8,8,128]{3,2,1,0:T(8,128)} copy(f32[64,8,8,128]{3,1,2,0:T(8,128)} %get-tuple-element.85) | data formatting | bytes 4194304
  46.3 2.9 %copy.94 = f32[4,128,1,8,128]{1,4,3,0,2:T(8,128)} copy(f32[4,128,1,8,128]{4,3,2,1,0:T(8,128)} %bitcast.434) | data formatting | bytes 4194304 | tf_op jit(solution)/shard_map/convert_element_type | solution.py:97
  49.2 1.0 broadcast_and_fusion.1
  50.2 1.0 fusion.83
  51.2 2.1 %collective-permute-start.3 = (bf16[1,2,512,128]{3,2,1,0:T(8,128)(2,1)S(1)}, bf16[1,2,512,128]{3,2,1,0:T(8,128)(2,1)S(1)}, u32[]{:S(2)}, u32[]{:S(2)}) collective-permute-start(bf16[1,2,512,128]{3,2,1,0:T(8,128)(2,1)S(1)} %get-tuple-element.135), channel_id=1, source_target_pairs={{0,4},{4,8},{8,12},{12,16},{16,20},{20,24},{24,28},{28,32},{32,36}... | collective-permute-start | bytes 786440 | tf_op jit(solution)/shard_map/ppermute | solution.py:41
  53.8 1.6 %fusion.6 = (f32[4,8,128]{2,1,0:T(8,128)S(1)}, f32[4,640,128,8]{2,1,3,0:T(8,128)S(1)}) fusion(pred[4,128,640]{1,2,0:T(8,128)(4,1)S(1)} %get-tuple-element.152, bf16[4,128,8,128]{3,2,1,0:T(8,128)(2,1)S(1)} %bitcast.431, bf16[4,640,1,128]{3,1,0,2:T(8,128)(2,1)S(1)} %constant_dynamic-update-slice_fusion.10), kind=kOutput, calls=%fused_computation.11 | convolution fusion | flops 678948864 | bytes 12533760 | tf_op jit(solution)/shard_map/btgjd,bkgd->bgjtk/dot_general | solution.py:87
  55.5 2.4 %fusion.15 = f32[4,8,128]{2,1,0:T(8,128)S(1)} fusion(f32[4,640,128,8]{2,1,3,0:T(8,128)S(1)} %get-tuple-element.156, f32[4,8,128]{2,1,0:T(8,128)S(1)} %get-tuple-element.155, pred[4,128,640]{1,2,0:T(8,128)(4,1)S(1)} %get-tuple-element.152), kind=kLoop, calls=%fused_computation.22 | loop fusion | flops 10481664 | bytes 10846208 | tf_op jit(solution)/shard_map/reduce_sum | solution.py:92
  57.9 3.1 %fusion.41 = f32[4,640,1,128]{3,1,0,2:T(8,128)S(1)} fusion(bf16[4,128,8,128]{3,2,1,0:T(8,128)(2,1)S(1)} %bitcast.458, f32[4,8,128]{2,1,0:T(8,128)S(1)} %fusion.15, f32[4,8,128]{2,1,0:T(8,128)S(1)} %get-tuple-element.155, f32[4,640,128,8]{2,1,3,0:T(8,128)S(1)} %get-tuple-element.156, pred[4,128,640]{1,2,0:T(8,128)(4,1)S(1)} %get-tuple-element.152), kind=kOutput, calls=%fused_computation.51 | convolution fusion | flops 684195840 | bytes 13205504 | tf_op jit(solution)/shard_map/bgjtk,btgjd->bkgd/dot_general | solution.py:110
  61.1 3.2 %fusion.29 = f32[4,128,8]{1,2,0:T(8,128)S(1)} fusion(f32[4,128,1,8,128]{1,4,3,0,2:T(8,128)S(1)} %copy-done.3, bf16[4,640,1,128]{3,1,0,2:T(8,128)(2,1)S(1)} %constant_dynamic-update-slice_fusion.15, f32[4,8,128]{2,1,0:T(8,128)S(1)} %fusion.15, f32[4,8,128]{2,1,0:T(8,128)S(1)} %get-tuple-element.155, f32[4,640,128,8]{2,1,3,0:T(8,128)S(1)} %get-tuple-element.156, ...), kind=kOutput, calls=%fused_computation.38 | convolution fusion | flops 686288896 | bytes 13615104 | tf_op jit(solution)/shard_map/bgjtk,bkgd->btgjd/dot_general | solution.py:94
  64.2 4.2 %fusion.17 = bf16[4,8,128,640]{2,3,1,0:T(8,128)(2,1)S(1)} fusion(f32[4,8,128]{2,1,0:T(8,128)S(1)} %bitcast.492, f32[4,8,128]{2,1,0:T(8,128)S(1)} %fusion.15, f32[4,8,128]{2,1,0:T(8,128)S(1)} %get-tuple-element.155, f32[4,640,128,8]{2,1,3,0:T(8,128)S(1)} %get-tuple-element.156, pred[4,128,640]{1,2,0:T(8,128)(4,1)S(1)} %get-tuple-element.152, ...), kind=kOutput, calls=%fused_computation.24 | convolution fusion | flops 692060160 | bytes 17809408 | tf_op jit(solution)/shard_map/btgjd,bkgd->bgjtk/dot_general | solution.py:98
  68.7 1.5 %convolution_bitcast_fusion = f32[4,640,1,128]{3,1,0,2:T(8,128)S(1)} fusion(bf16[4,8,128,640]{2,3,1,0:T(8,128)(2,1)S(1)} %fusion.17, bf16[4,128,8,128]{3,2,1,0:T(8,128)(2,1)S(1)} %bitcast.432), kind=kOutput, calls=%fused_computation.48 | convolution fusion | flops 671088640 | bytes 7602176 | tf_op jit(solution)/shard_map/bgjtk,btgjd->bkgd/dot_general | solution.py:107
  70.5 2.1 %collective-permute-start.5 = (bf16[1,2,512,128]{3,2,1,0:T(8,128)(2,1)S(1)}, bf16[1,2,512,128]{3,2,1,0:T(8,128)(2,1)S(1)}, u32[]{:S(2)}, u32[]{:S(2)}) collective-permute-start(bf16[1,2,512,128]{3,2,1,0:T(8,128)(2,1)S(1)} %fusion.76), channel_id=1, source_target_pairs={{0,4},{4,8},{8,12},{12,16},{16,20},{20,24},{24,28},{28,32},{32,36}... | collective-permute-start | bytes 786440 | tf_op jit(solution)/shard_map/ppermute | solution.py:41
  73.2 1.6 %fusion.9 = (f32[4,8,128]{2,1,0:T(8,128)S(1)}, f32[4,640,128,8]{2,1,3,0:T(8,128)S(1)}) fusion(pred[4,128,640]{1,2,0:T(8,128)(4,1)S(1)} %get-tuple-element.151, bf16[4,128,8,128]{3,2,1,0:T(8,128)(2,1)S(1)} %bitcast.429, bf16[4,640,1,128]{3,1,0,2:T(8,128)(2,1)S(1)} %constant_dynamic-update-slice_fusion), kind=kOutput, calls=%fused_computation.16 | convolution fusion | flops 678948864 | bytes 12533760 | tf_op jit(solution)/shard_map/btgjd,bkgd->bgjtk/dot_general | solution.py:87
  74.8 2.4 %fusion.13 = f32[4,8,128]{2,1,0:T(8,128)S(1)} fusion(f32[4,640,128,8]{2,1,3,0:T(8,128)S(1)} %get-tuple-element.158, f32[4,8,128]{2,1,0:T(8,128)S(1)} %get-tuple-element.157, pred[4,128,640]{1,2,0:T(8,128)(4,1)S(1)} %get-tuple-element.151), kind=kLoop, calls=%fused_computation.20 | loop fusion | flops 10481664 | bytes 10846208 | tf_op jit(solution)/shard_map/reduce_sum | solution.py:92
  77.3 3.1 %fusion.38 = f32[4,640,1,128]{3,1,0,2:T(8,128)S(1)} fusion(bf16[4,128,8,128]{3,2,1,0:T(8,128)(2,1)S(1)} %bitcast.456, f32[4,8,128]{2,1,0:T(8,128)S(1)} %fusion.13, f32[4,8,128]{2,1,0:T(8,128)S(1)} %get-tuple-element.157, f32[4,640,128,8]{2,1,3,0:T(8,128)S(1)} %get-tuple-element.158, pred[4,128,640]{1,2,0:T(8,128)(4,1)S(1)} %get-tuple-element.151), kind=kOutput, calls=%fused_computation.50 | convolution fusion | flops 684195840 | bytes 13205504 | tf_op jit(solution)/shard_map/bgjtk,btgjd->bkgd/dot_general | solution.py:110
  80.4 3.2 %fusion.31 = f32[4,128,8]{1,2,0:T(8,128)S(1)} fusion(f32[4,128,1,8,128]{1,4,3,0,2:T(8,128)S(1)} %copy-done.2, bf16[4,640,1,128]{3,1,0,2:T(8,128)(2,1)S(1)} %constant_dynamic-update-slice_fusion.5, f32[4,8,128]{2,1,0:T(8,128)S(1)} %fusion.13, f32[4,8,128]{2,1,0:T(8,128)S(1)} %get-tuple-element.157, f32[4,640,128,8]{2,1,3,0:T(8,128)S(1)} %get-tuple-element.158, ...), kind=kOutput, calls=%fused_computation.41 | convolution fusion | flops 686288896 | bytes 13615104 | tf_op jit(solution)/shard_map/bgjtk,bkgd->btgjd/dot_general | solution.py:94
  83.6 4.2 %fusion.16 = bf16[4,8,128,640]{2,3,1,0:T(8,128)(2,1)S(1)} fusion(f32[4,8,128]{2,1,0:T(8,128)S(1)} %bitcast.493, f32[4,8,128]{2,1,0:T(8,128)S(1)} %fusion.13, f32[4,8,128]{2,1,0:T(8,128)S(1)} %get-tuple-element.157, f32[4,640,128,8]{2,1,3,0:T(8,128)S(1)} %get-tuple-element.158, pred[4,128,640]{1,2,0:T(8,128)(4,1)S(1)} %get-tuple-element.151, ...), kind=kOutput, calls=%fused_computation.23 | convolution fusion | flops 692060160 | bytes 17809408 | tf_op jit(solution)/shard_map/btgjd,bkgd->bgjtk/dot_general | solution.py:98
  88.0 1.5 %convolution_bitcast_fusion.1 = f32[4,640,1,128]{3,1,0,2:T(8,128)S(1)} fusion(bf16[4,8,128,640]{2,3,1,0:T(8,128)(2,1)S(1)} %fusion.16, bf16[4,128,8,128]{3,2,1,0:T(8,128)(2,1)S(1)} %bitcast.430), kind=kOutput, calls=%fused_computation.49 | convolution fusion | flops 671088640 | bytes 7602176 | tf_op jit(solution)/shard_map/bgjtk,btgjd->bkgd/dot_general | solution.py:107
  89.8 5.8 %collective-permute-start.6 = (bf16[1,2,512,128]{3,2,1,0:T(8,128)(2,1)S(1)}, bf16[1,2,512,128]{3,2,1,0:T(8,128)(2,1)S(1)}, u32[]{:S(2)}, u32[]{:S(2)}) collective-permute-start(bf16[1,2,512,128]{3,2,1,0:T(8,128)(2,1)S(1)} %maximum_bitcast_fusion.3), channel_id=1, source_target_pairs={{4,0},{8,4},{12,8},{16,12},{20,16},{24,20},{28,24},{32,28},{36,32}... | collective-permute-start | bytes 786440 | tf_op jit(solution)/shard_map/ppermute | solution.py:43
  95.6 3.9 %collective-permute-done.6 = bf16[1,2,512,128]{3,2,1,0:T(8,128)(2,1)S(1)} collective-permute-done((bf16[1,2,512,128]{3,2,1,0:T(8,128)(2,1)S(1)}, bf16[1,2,512,128]{3,2,1,0:T(8,128)(2,1)S(1)}, u32[]{:S(2)}, u32[]{:S(2)}) %collective-permute-start.6) | collective-permute-done | bytes 262176 | tf_op jit(solution)/shard_map/ppermute | solution.py:43
  99.7 1.0 copy.104
  100.6 4.8 %all-to-all-start.2 = ((bf16[1,2,512,128]{3,1,0,2:T(2,128)(2,1)}), bf16[1,2,512,128]{3,1,0,2:T(2,128)(2,1)S(1)}, u32[]{:S(2)}, u32[]{:S(2)}) async-start(bf16[1,2,512,128]{3,1,0,2:T(2,128)(2,1)} %copy.104), calls=%async_computation.2 | async-start | bytes 524288 | tf_op jit(solution)/shard_map/all_to_all | solution.py:187
  105.4 4.5 %fusion.45 = bf16[4,128,1,8,128]{1,4,3,0,2:T(8,128)(2,1)} fusion(bf16[4,8,128,640]{2,3,1,0:T(8,128)(2,1)} %copy-done, bf16[4,640,1,128]{3,1,0,2:T(8,128)(2,1)S(1)} %constant_dynamic-update-slice_fusion.10), kind=kOutput, calls=%fused_computation.53 | convolution fusion | flops 671612928 | bytes 6946816 | tf_op jit(solution)/shard_map/bgjtk,bkgd->btgjd/dot_general | solution.py:104
  109.9 1.7 %copy.97 = bf16[4,128,1,8,128]{4,3,1,0,2:T(8,128)(2,1)S(1)} copy(bf16[4,128,1,8,128]{1,4,3,0,2:T(8,128)(2,1)} %fusion.45) | data formatting | bytes 2097152 | tf_op jit(solution)/shard_map/convert_element_type | solution.py:106
  112.2 1.0 copy.102
  113.1 4.8 %all-to-all-start.1 = ((bf16[1,2,512,128]{3,1,0,2:T(2,128)(2,1)}), bf16[1,2,512,128]{3,1,0,2:T(2,128)(2,1)S(1)}, u32[]{:S(2)}, u32[]{:S(2)}) async-start(bf16[1,2,512,128]{3,1,0,2:T(2,128)(2,1)} %copy.102), calls=%async_computation.1 | async-start | bytes 524288 | tf_op jit(solution)/shard_map/all_to_all | solution.py:186
  117.9 4.5 %fusion.44 = bf16[4,128,1,8,128]{1,4,3,0,2:T(8,128)(2,1)} fusion(bf16[4,8,128,640]{2,3,1,0:T(8,128)(2,1)} %copy-done.1, bf16[4,640,1,128]{3,1,0,2:T(8,128)(2,1)S(1)} %constant_dynamic-update-slice_fusion), kind=kOutput, calls=%fused_computation.52 | convolution fusion | flops 671612928 | bytes 6946816 | tf_op jit(solution)/shard_map/bgjtk,bkgd->btgjd/dot_general | solution.py:104
  122.4 1.7 %copy.89 = bf16[4,128,1,8,128]{4,3,1,0,2:T(8,128)(2,1)S(1)} copy(bf16[4,128,1,8,128]{1,4,3,0,2:T(8,128)(2,1)} %fusion.44) | data formatting | bytes 2097152 | tf_op jit(solution)/shard_map/convert_element_type | solution.py:106
  124.1 1.3 stack_reshape.6
  125.4 2.7 %maximum_bitcast_fusion = bf16[1,2,512,1024]{3,2,1,0:T(8,128)(2,1)} fusion(bf16[1,512,1024]{2,1,0:T(8,128)(2,1)S(1)} %stack_reshape.7, bf16[1,512,1024]{2,1,0:T(8,128)(2,1)} %stack_reshape.6), kind=kLoop, calls=%fused_computation.35 | loop fusion | flops 1048576 | bytes 4194304 | tf_op jit(solution)/shard_map/broadcast_in_dim | solution.py:182
  128.3 0.8 all_to_all.50
  129.3 0.8 all_to_all.46
  (109 shorter events, 6.0 us)
Async XLA Ops:
  1.9 20.2 %collective-permute-start = (bf16[1,2,128,128]{3,2,1,0:T(8,128)(2,1)S(1)}, bf16[1,2,128,128]{3,2,1,0:T(8,128)(2,1)S(1)}, u32[]{:S(2)}, u32[]{:S(2)}) collective-permute-start(bf16[1,2,128,128]{3,2,1,0:T(8,128)(2,1)S(1)} %bitcast.486), channel_id=1, source_target_pairs={{0,1},{1,0},{2,3},{3,2},{4,5},{5,4},{6,7},{7,6},{8,9},{9,8},{10,11... | collective-permute-start | bytes 196616 | tf_op jit(solution)/shard_map/ppermute | solution.py:28
  2.7 19.5 %collective-permute-start.1 = (bf16[1,2,128,128]{3,2,1,0:T(8,128)(2,1)S(1)}, bf16[1,2,128,128]{3,2,1,0:T(8,128)(2,1)S(1)}, u32[]{:S(2)}, u32[]{:S(2)}) collective-permute-start(bf16[1,2,128,128]{3,2,1,0:T(8,128)(2,1)S(1)} %bitcast.487), channel_id=1, source_target_pairs={{0,2},{1,3},{2,0},{3,1},{4,6},{5,7},{6,4},{7,5},{8,10},{9,11},{10,... | collective-permute-start | bytes 196616 | tf_op jit(solution)/shard_map/ppermute | solution.py:28
  5.3 16.8 %collective-permute-start.2 = (bf16[1,2,128,128]{3,2,1,0:T(8,128)(2,1)S(1)}, bf16[1,2,128,128]{3,2,1,0:T(8,128)(2,1)S(1)}, u32[]{:S(2)}, u32[]{:S(2)}) collective-permute-start(bf16[1,2,128,128]{3,2,1,0:T(8,128)(2,1)S(1)} %bitcast.488), channel_id=1, source_target_pairs={{0,3},{1,2},{2,1},{3,0},{4,7},{5,6},{6,5},{7,4},{8,11},{9,10},{10,... | collective-permute-start | bytes 196616 | tf_op jit(solution)/shard_map/ppermute | solution.py:28
  7.8 15.1 %all-to-all-start = ((bf16[1,2,128,512]{2,1,0,3:T(2,128)(2,1)}), bf16[1,2,128,512]{2,1,0,3:T(2,128)(2,1)S(1)}, u32[]{:S(2)}, u32[]{:S(2)}) async-start(bf16[1,2,128,512]{2,1,0,3:T(2,128)(2,1)} %copy.80), calls=%async_computation | async-start | bytes 524288 | tf_op jit(solution)/shard_map/all_to_all | solution.py:123
  24.8 25.4 %collective-permute-start.4 = (bf16[1,2,512,128]{3,2,1,0:T(8,128)(2,1)}, bf16[1,2,512,128]{3,2,1,0:T(8,128)(2,1)}, u32[]{:S(2)}, u32[]{:S(2)}) collective-permute-start(bf16[1,2,512,128]{3,2,1,0:T(8,128)(2,1)} %maximum_bitcast_fusion.2), channel_id=1, source_target_pairs={{4,0},{8,4},{12,8},{16,12},{20,16},{24,20},{28,24},{32,28},{36,32}... | collective-permute-start | bytes 786440 | tf_op jit(solution)/shard_map/ppermute | solution.py:43
  31.4 17.8 %copy-start.13 = (pred[128,640]{0,1:T(8,128)(4,1)S(1)}, pred[128,640]{0,1:T(8,128)(4,1)}, u32[]{:S(2)}) copy-start(pred[128,640]{0,1:T(8,128)(4,1)} %iota_compare_fusion) | copy-start | bytes 245764
  31.4 18.8 %copy-start.11 = (bf16[1,512,128]{2,1,0:T(8,128)(2,1)S(1)}, bf16[1,512,128]{2,1,0:T(8,128)(2,1)}, u32[]{:S(2)}) copy-start(bf16[1,512,128]{2,1,0:T(8,128)(2,1)} %get-tuple-element.114) | copy-start | bytes 393220
  31.4 18.8 %copy-start.12 = (bf16[1,512,128]{2,1,0:T(8,128)(2,1)S(1)}, bf16[1,512,128]{2,1,0:T(8,128)(2,1)}, u32[]{:S(2)}) copy-start(bf16[1,512,128]{2,1,0:T(8,128)(2,1)} %get-tuple-element.163) | copy-start | bytes 393220
  34.0 19.4 %copy-start.6 = (bf16[512,128]{1,0:T(8,128)(2,1)S(1)}, bf16[512,128]{1,0:T(8,128)(2,1)}, u32[]{:S(2)}) copy-start(bf16[512,128]{1,0:T(8,128)(2,1)} %get-tuple-element.117) | copy-start | bytes 393220
  36.6 17.1 %copy-start.10 = (bf16[1,1,512,128]{3,2,1,0:T(8,128)(2,1)S(1)}, bf16[1,1,512,128]{3,2,1,0:T(8,128)(2,1)}, u32[]{:S(2)}) copy-start(bf16[1,1,512,128]{3,2,1,0:T(8,128)(2,1)} %get-tuple-element.159) | copy-start | bytes 393220
  40.0 13.8 %copy-start.9 = (bf16[1,1,512,128]{3,2,1,0:T(8,128)(2,1)S(1)}, bf16[1,1,512,128]{3,2,1,0:T(8,128)(2,1)}, u32[]{:S(2)}) copy-start(bf16[1,1,512,128]{3,2,1,0:T(8,128)(2,1)} %get-tuple-element.118) | copy-start | bytes 393220
  51.2 21.5 %collective-permute-start.3 = (bf16[1,2,512,128]{3,2,1,0:T(8,128)(2,1)S(1)}, bf16[1,2,512,128]{3,2,1,0:T(8,128)(2,1)S(1)}, u32[]{:S(2)}, u32[]{:S(2)}) collective-permute-start(bf16[1,2,512,128]{3,2,1,0:T(8,128)(2,1)S(1)} %get-tuple-element.135), channel_id=1, source_target_pairs={{0,4},{4,8},{8,12},{12,16},{16,20},{20,24},{24,28},{28,32},{32,36}... | collective-permute-start | bytes 786440 | tf_op jit(solution)/shard_map/ppermute | solution.py:41
  53.8 4.1 %copy-start.5 = (bf16[64,8,8,128]{3,2,1,0:T(8,128)(2,1)S(1)}, bf16[64,8,8,128]{3,2,1,0:T(8,128)(2,1)}, u32[]{:S(2)}) copy-start(bf16[64,8,8,128]{3,2,1,0:T(8,128)(2,1)} %copy.136) | copy-start | bytes 3145732
  57.9 3.1 %copy-start.3 = (f32[4,128,1,8,128]{1,4,3,0,2:T(8,128)S(1)}, f32[4,128,1,8,128]{1,4,3,0,2:T(8,128)}, u32[]{:S(2)}) copy-start(f32[4,128,1,8,128]{1,4,3,0,2:T(8,128)} %copy.94) | copy-start | bytes 6291460
  68.5 4.4 %copy-start = (bf16[4,8,128,640]{2,3,1,0:T(8,128)(2,1)}, bf16[4,8,128,640]{2,3,1,0:T(8,128)(2,1)S(1)}, u32[]{:S(2)}) copy-start(bf16[4,8,128,640]{2,3,1,0:T(8,128)(2,1)S(1)} %fusion.17) | copy-start | bytes 15728644
  68.5 4.5 %copy-start.8 = (bf16[1,1,512,128]{3,2,1,0:T(8,128)(2,1)S(1)}, bf16[1,1,512,128]{3,2,1,0:T(8,128)(2,1)}, u32[]{:S(2)}) copy-start(bf16[1,1,512,128]{3,2,1,0:T(8,128)(2,1)} %get-tuple-element.164) | copy-start | bytes 393220
  68.6 4.5 %copy-start.7 = (bf16[1,1,512,128]{3,2,1,0:T(8,128)(2,1)S(1)}, bf16[1,1,512,128]{3,2,1,0:T(8,128)(2,1)}, u32[]{:S(2)}) copy-start(bf16[1,1,512,128]{3,2,1,0:T(8,128)(2,1)} %get-tuple-element.113) | copy-start | bytes 393220
  70.5 25.0 %collective-permute-start.5 = (bf16[1,2,512,128]{3,2,1,0:T(8,128)(2,1)S(1)}, bf16[1,2,512,128]{3,2,1,0:T(8,128)(2,1)S(1)}, u32[]{:S(2)}, u32[]{:S(2)}) collective-permute-start(bf16[1,2,512,128]{3,2,1,0:T(8,128)(2,1)S(1)} %fusion.76), channel_id=1, source_target_pairs={{0,4},{4,8},{8,12},{12,16},{16,20},{20,24},{24,28},{28,32},{32,36}... | collective-permute-start | bytes 786440 | tf_op jit(solution)/shard_map/ppermute | solution.py:41
  73.2 4.1 %copy-start.4 = (bf16[64,8,8,128]{3,2,1,0:T(8,128)(2,1)S(1)}, bf16[64,8,8,128]{3,2,1,0:T(8,128)(2,1)}, u32[]{:S(2)}) copy-start(bf16[64,8,8,128]{3,2,1,0:T(8,128)(2,1)} %copy.133) | copy-start | bytes 3145732
  77.3 3.1 %copy-start.2 = (f32[4,128,1,8,128]{1,4,3,0,2:T(8,128)S(1)}, f32[4,128,1,8,128]{1,4,3,0,2:T(8,128)}, u32[]{:S(2)}) copy-start(f32[4,128,1,8,128]{1,4,3,0,2:T(8,128)} %copy.86) | copy-start | bytes 6291460
  87.8 11.7 %copy-start.1 = (bf16[4,8,128,640]{2,3,1,0:T(8,128)(2,1)}, bf16[4,8,128,640]{2,3,1,0:T(8,128)(2,1)S(1)}, u32[]{:S(2)}) copy-start(bf16[4,8,128,640]{2,3,1,0:T(8,128)(2,1)S(1)} %fusion.16) | copy-start | bytes 15728644
  89.8 9.6 %collective-permute-start.6 = (bf16[1,2,512,128]{3,2,1,0:T(8,128)(2,1)S(1)}, bf16[1,2,512,128]{3,2,1,0:T(8,128)(2,1)S(1)}, u32[]{:S(2)}, u32[]{:S(2)}) collective-permute-start(bf16[1,2,512,128]{3,2,1,0:T(8,128)(2,1)S(1)} %maximum_bitcast_fusion.3), channel_id=1, source_target_pairs={{4,0},{8,4},{12,8},{16,12},{20,16},{24,20},{28,24},{32,28},{36,32}... | collective-permute-start | bytes 786440 | tf_op jit(solution)/shard_map/ppermute | solution.py:43
  100.6 12.5 %all-to-all-start.2 = ((bf16[1,2,512,128]{3,1,0,2:T(2,128)(2,1)}), bf16[1,2,512,128]{3,1,0,2:T(2,128)(2,1)S(1)}, u32[]{:S(2)}, u32[]{:S(2)}) async-start(bf16[1,2,512,128]{3,1,0,2:T(2,128)(2,1)} %copy.104), calls=%async_computation.2 | async-start | bytes 524288 | tf_op jit(solution)/shard_map/all_to_all | solution.py:187
  113.1 16.0 %all-to-all-start.1 = ((bf16[1,2,512,128]{3,1,0,2:T(2,128)(2,1)}), bf16[1,2,512,128]{3,1,0,2:T(2,128)(2,1)S(1)}, u32[]{:S(2)}, u32[]{:S(2)}) async-start(bf16[1,2,512,128]{3,1,0,2:T(2,128)(2,1)} %copy.102), calls=%async_computation.1 | async-start | bytes 524288 | tf_op jit(solution)/shard_map/all_to_all | solution.py:186
